TPU v7x, 32 devices: a whole 2x2x4 slice. The times are simulated.
32 devices in a mesh: dp: 8 (over y, x, core), tensor: 4 (over z).
Axes of the slice: x: 2, y: 2, z: 4, core: 2. Of those that a mesh axis runs over, the one named last changes fastest.
Arguments:
- tokens: bfloat16 [16384, 768], P(('dp', 'tensor')), may hold values from -6 to 6
- starts: int32 [8, 8], P('dp'), may hold values from 0 to 2047, as said below
- w_qkv: bfloat16 [768, 2304], P(None, 'tensor'), may hold values from -0.21875 to 0.21875
- b_qkv: bfloat16 [2304], P('tensor'), may hold values from -3 to 3
- w_out: bfloat16 [768, 768], P('tensor'), may hold values from -2 to 2
- b_out: bfloat16 [768], replicated, may hold values from -3 to 3
- gain_one: bfloat16 [768], replicated, may hold values from 0.099609375 to 1.8984375
- shift_one: bfloat16 [768], replicated, may hold values from -3 to 3
- w_in: bfloat16 [768, 3072], P(None, 'tensor'), may hold values from -0.21875 to 0.21875
- b_in: bfloat16 [3072], P('tensor'), may hold values from -3 to 3
- w_two: bfloat16 [3072, 768], P('tensor'), may hold values from -0.21875 to 0.21875
- b_two: bfloat16 [768], replicated, may hold values from -3 to 3
- gain_two: bfloat16 [768], replicated, may hold values from 0.099609375 to 1.8984375
- shift_two: bfloat16 [768], replicated, may hold values from -3 to 3
- cotangent: bfloat16 [16384, 768], P(('dp', 'tensor')), may hold values from -6 to 6
Outputs:
- block_out: bfloat16 [16384, 768], P(('dp', 'tensor'))
- d_tokens: bfloat16 [16384, 768], P(('dp', 'tensor'))
- d_w_qkv: float32 [768, 2304], P(None, 'tensor')
- d_b_qkv: float32 [2304], P('tensor')
- d_w_out: float32 [768, 768], P('tensor')
- d_b_out: float32 [768], replicated
- d_gain_one: float32 [768], replicated
- d_shift_one: float32 [768], replicated
- d_w_in: float32 [768, 3072], P(None, 'tensor')
- d_b_in: float32 [3072], P('tensor')
- d_w_two: float32 [3072, 768], P('tensor')
- d_b_two: float32 [768], replicated
- d_gain_two: float32 [768], replicated
- d_shift_two: float32 [768], replicated
Inputs may be any that keep to these rules, and one draw needn't show every extreme that they name: Each row holds exactly 8 documents: its first start is 0 and its starts rise strictly. In the first row the last document is a single token.
All inputs are finite; a program needn't handle non-finite values.
Results may differ from a plain program's by a relative error of at most 0.014.
Values may be sent and summed in bfloat16 or wider, within the bound.
No kernel may reach another device: no remote copies, remote signals or barrier semaphores. Data moves between devices by JAX's collectives and lax.ppermute only.
A program may use at most 192 MiB of HBM per device.

v0:
```python
import math
import jax
import jax.numpy as jnp
from jax import lax
from jax.sharding import PartitionSpec as P

HEAD = 64
GROUP = 64
ROW_LEN = 2048
DOCS = 8
highest = lax.Precision.HIGHEST


def doc_tables(starts_row):
    places = jnp.arange(ROW_LEN, dtype=jnp.int32)
    started = (places[:, None] >= starts_row[None, :]).astype(jnp.int32)
    doc_ids = jnp.sum(started, axis=1) - 1
    onehot = (doc_ids[:, None] == jnp.arange(DOCS, dtype=jnp.int32)[None, :]).astype(jnp.int32)
    finish = jnp.concatenate([starts_row[1:], jnp.full((1,), ROW_LEN, jnp.int32)])
    own_start = jnp.sum(onehot * starts_row[None, :], axis=1)
    own_len = jnp.sum(onehot * (finish - starts_row)[None, :], axis=1)
    angles = 0.5 * math.pi * (places - own_start).astype(jnp.float32) / own_len.astype(jnp.float32)
    return (angles, doc_ids)


def attend(mixed, angles, doc_ids):
    length = mixed.shape[0]
    head_count = mixed.shape[1] // (3 * HEAD)
    blocks = length // GROUP
    pieces = mixed.reshape(blocks, GROUP, head_count, 3, HEAD)
    queries = jax.nn.relu(pieces[:, :, :, 0])
    key_pos = jax.nn.relu(pieces[:, :, :, 1])
    values = pieces[:, :, :, 2]
    cosine = jnp.cos(angles).reshape(blocks, GROUP, 1, 1)
    sines = jnp.sin(angles).reshape(blocks, GROUP, 1, 1)
    query_feat = jnp.concatenate([queries * cosine, queries * sines], axis=-1)
    key_feat = jnp.concatenate([key_pos * cosine, key_pos * sines], axis=-1)
    doc_blocks = doc_ids.reshape(blocks, GROUP)
    within = jnp.arange(GROUP, dtype=jnp.int32)
    inside_mask = (
        (doc_blocks[:, :, None] == doc_blocks[:, None, :])
        & (within[None, :, None] >= within[None, None, :])
    ).astype(jnp.float32)
    scores = (
        jnp.einsum("bihf,bjhf->bhij", query_feat, key_feat, precision=highest)
        * inside_mask[:, None]
    )
    numerator = jnp.einsum("bhij,bjhd->bihd", scores, values, precision=highest)
    denominator = jnp.transpose(jnp.sum(scores, axis=-1), (0, 2, 1))
    first_doc = doc_blocks[:, 0]
    last_doc = doc_blocks[:, -1]
    tail_mask = (doc_blocks == last_doc[:, None]).astype(jnp.float32)
    states = jnp.einsum("bjhf,bjhd,bj->bhfd", key_feat, values, tail_mask, precision=highest)
    key_sums = jnp.einsum("bjhf,bj->bhf", key_feat, tail_mask, precision=highest)
    order = jnp.arange(blocks, dtype=jnp.int32)
    link_mask = (
        (last_doc[None, :] == first_doc[:, None]) & (order[None, :] < order[:, None])
    ).astype(jnp.float32)
    carried = jnp.einsum("cb,bhfd->chfd", link_mask, states, precision=highest)
    carried_sum = jnp.einsum("cb,bhf->chf", link_mask, key_sums, precision=highest)
    opening = (doc_blocks == first_doc[:, None]).astype(jnp.float32)
    numerator = numerator + jnp.einsum(
        "bihf,bhfd,bi->bihd", query_feat, carried, opening, precision=highest
    )
    denominator = denominator + jnp.einsum(
        "bihf,bhf,bi->bih", query_feat, carried_sum, opening, precision=highest
    )
    result = numerator / jnp.maximum(denominator, 1.0)[..., None]
    return result.reshape(length, head_count * HEAD)


def attend_rows(mixed, angles, doc_ids):
    row_count = angles.shape[0]
    shaped = mixed.reshape(row_count, angles.shape[1], mixed.shape[1])
    return jax.vmap(attend)(shaped, angles, doc_ids).reshape(mixed.shape[0], -1)


def normalize(rows_in, gain, shift):
    centred = rows_in - jnp.mean(rows_in, axis=-1, keepdims=True)
    spread = jnp.mean(centred * centred, axis=-1, keepdims=True)
    return centred * lax.rsqrt(spread + 1e-05) * gain + shift


def smooth(values):
    return jax.nn.gelu(values)


def inner_rows(left, right):
    return lax.dot_general(
        left, right, (((0,), (0,)), ((), ())), preferred_element_type=jnp.float32
    )


def times_rows(left, right):
    return lax.dot_general(
        left, right, (((1,), (1,)), ((), ())), preferred_element_type=jnp.float32
    )


def rows_product(source, weight):
    return jnp.dot(source, weight, preferred_element_type=jnp.float32)


def rows_back(source, weight):
    return times_rows(source, weight)


def on_device(
    tokens,
    starts,
    w_qkv,
    b_qkv,
    w_out,
    b_out,
    gain_one,
    shift_one,
    w_in,
    b_in,
    w_two,
    b_two,
    gain_two,
    shift_two,
    cotangent,
):
    angles, doc_ids = jax.vmap(doc_tables)(starts)
    bias_qkv = b_qkv.astype(jnp.float32)
    bias_in = b_in.astype(jnp.float32)
    gain_a = gain_one.astype(jnp.float32)
    shift_a = shift_one.astype(jnp.float32)
    gain_b = gain_two.astype(jnp.float32)
    shift_b = shift_two.astype(jnp.float32)
    input_full = lax.all_gather(tokens, "tensor", axis=0, tiled=True)
    mixed = jnp.dot(input_full, w_qkv, preferred_element_type=jnp.float32) + bias_qkv
    attended = attend_rows(mixed, angles, doc_ids).astype(jnp.bfloat16)
    branch = lax.psum_scatter(
        rows_product(attended, w_out), "tensor", scatter_dimension=0, tiled=True
    ) + b_out.astype(jnp.float32)
    first_sum = tokens.astype(jnp.float32) + branch
    first_low = normalize(first_sum, gain_a, shift_a).astype(jnp.bfloat16)
    middle_full = lax.all_gather(first_low, "tensor", axis=0, tiled=True)
    hidden = jnp.dot(middle_full, w_in, preferred_element_type=jnp.float32) + bias_in
    active = smooth(hidden).astype(jnp.bfloat16)
    second = lax.psum_scatter(
        rows_product(active, w_two), "tensor", scatter_dimension=0, tiled=True
    ) + b_two.astype(jnp.float32)
    second_sum = first_low.astype(jnp.float32) + second
    block_out = normalize(second_sum, gain_b, shift_b).astype(jnp.bfloat16)
    input_back = lax.all_gather(tokens, "tensor", axis=0, tiled=True)
    middle_back = lax.all_gather(first_low, "tensor", axis=0, tiled=True)
    unused_two, norm_two_back = jax.vjp(normalize, second_sum, gain_b, shift_b)
    d_r2, d_gain_two, d_shift_two = norm_two_back(cotangent.astype(jnp.float32))
    d_second = d_r2.astype(jnp.bfloat16)
    d_b_two = jnp.sum(d_second, axis=0, dtype=jnp.float32)
    second_full = lax.all_gather(d_second, "tensor", axis=0, tiled=True)
    hidden_again = jnp.dot(middle_back, w_in, preferred_element_type=jnp.float32) + bias_in
    active_val, gelu_back = jax.vjp(smooth, hidden_again)
    active_again = active_val.astype(jnp.bfloat16)
    d_w_two = inner_rows(active_again, second_full)
    d_active = times_rows(second_full, w_two)
    d_hidden = gelu_back(d_active)[0].astype(jnp.bfloat16)
    d_b_in = jnp.sum(d_hidden, axis=0, dtype=jnp.float32)
    d_w_in = inner_rows(middle_back, d_hidden)
    d_first = (
        lax.psum_scatter(rows_back(d_hidden, w_in), "tensor", scatter_dimension=0, tiled=True)
        + d_r2
    )
    unused_one, norm_one_back = jax.vjp(normalize, first_sum, gain_a, shift_a)
    d_r1, d_gain_one, d_shift_one = norm_one_back(d_first)
    d_branch = d_r1.astype(jnp.bfloat16)
    d_b_out = jnp.sum(d_branch, axis=0, dtype=jnp.float32)
    branch_full = lax.all_gather(d_branch, "tensor", axis=0, tiled=True)
    mixed_again = jnp.dot(input_back, w_qkv, preferred_element_type=jnp.float32) + bias_qkv
    attended_val, attend_back = jax.vjp(
        lambda mixed_in: attend_rows(mixed_in, angles, doc_ids), mixed_again
    )
    attended_again = attended_val.astype(jnp.bfloat16)
    d_w_out = inner_rows(attended_again, branch_full)
    d_attended = times_rows(branch_full, w_out)
    d_mixed = attend_back(d_attended)[0].astype(jnp.bfloat16)
    d_b_qkv = jnp.sum(d_mixed, axis=0, dtype=jnp.float32)
    d_w_qkv = inner_rows(input_back, d_mixed)
    d_tokens = (
        lax.psum_scatter(
            rows_back(d_mixed, w_qkv).astype(jnp.bfloat16),
            "tensor",
            scatter_dimension=0,
            tiled=True,
        ).astype(jnp.float32)
        + d_r1
    ).astype(jnp.bfloat16)
    d_w_qkv, d_b_qkv, d_w_out, d_w_in, d_b_in, d_w_two = lax.psum(
        (d_w_qkv, d_b_qkv, d_w_out, d_w_in, d_b_in, d_w_two), "dp"
    )
    d_b_out, d_gain_one, d_shift_one, d_b_two, d_gain_two, d_shift_two = lax.psum(
        (d_b_out, d_gain_one, d_shift_one, d_b_two, d_gain_two, d_shift_two), ("dp", "tensor")
    )
    return (
        block_out,
        d_tokens,
        d_w_qkv,
        d_b_qkv,
        d_w_out,
        d_b_out,
        d_gain_one,
        d_shift_one,
        d_w_in,
        d_b_in,
        d_w_two,
        d_b_two,
        d_gain_two,
        d_shift_two,
    )


def solution(mesh):
    in_specs = (
        P(("dp", "tensor"), None),
        P("dp", None),
        P(None, "tensor"),
        P("tensor"),
        P("tensor", None),
        P(),
        P(),
        P(),
        P(None, "tensor"),
        P("tensor"),
        P("tensor", None),
        P(),
        P(),
        P(),
        P(("dp", "tensor"), None),
    )
    out_specs = (
        P(("dp", "tensor"), None),
        P(("dp", "tensor"), None),
        P(None, "tensor"),
        P("tensor"),
        P("tensor", None),
        P(),
        P(),
        P(),
        P(None, "tensor"),
        P("tensor"),
        P("tensor", None),
        P(),
        P(),
        P(),
    )
    return jax.shard_map(
        on_device, mesh=mesh, in_specs=in_specs, out_specs=out_specs, check_vma=False
    )
```

profile of v0, /device:TPU:0, one launch (start us, length us, event | category | flops | bytes accessed | tf_op | source)
XLA Modules:
  0.0 1038.7 jit_solution(10530214980209661449)
XLA Ops:
  12.7 63.1 %all-gather.5.cloned.1.call-done = bf16[2048,768]{1,0:T(8,128)(2,1)} async-done(((bf16[512,768]{1,0:T(8,128)(2,1)}), bf16[2048,768]{1,0:T(8,128)(2,1)}) %all-gather.5.cloned.1.call-update) | async-done | bytes 3145744 | tf_op jit(solution)/shard_map/all_gather | solution.py:132
  82.2 8.7 reshape_reshape.3
  90.9 8.2 fusion.101
  150.5 9.1 divide_convert_fusion
  169.7 107.1 %reduce-scatter.5.cloned.1.call-done = f32[512,768]{1,0:T(8,128)} async-done(((f32[2048,768]{1,0:T(8,128)}), f32[512,768]{1,0:T(8,128)}) %reduce-scatter.5.cloned.1.call-update) | async-done | bytes 1572880 | tf_op jit(solution)/shard_map/reduce_scatter | solution.py:135
  280.2 64.1 %all-gather.7.cloned.1.call-done = bf16[2048,768]{1,0:T(8,128)(2,1)} async-done(((bf16[512,768]{1,0:T(8,128)(2,1)}), bf16[2048,768]{1,0:T(8,128)(2,1)}) %all-gather.7.cloned.1.call-update) | async-done | bytes 3145744 | tf_op jit(solution)/shard_map/all_gather | solution.py:140
  344.3 8.4 multiply_convert_fusion
  361.3 107.1 %reduce-scatter.7.cloned.1.call-done = f32[512,768]{1,0:T(8,128)} async-done(((f32[2048,768]{1,0:T(8,128)}), f32[512,768]{1,0:T(8,128)}) %reduce-scatter.7.cloned.1.call-update) | async-done | bytes 1572880 | tf_op jit(solution)/shard_map/reduce_scatter | solution.py:143
  476.5 64.1 %all-gather.9.cloned.1.call-done = bf16[2048,768]{1,0:T(8,128)(2,1)} async-done(((bf16[512,768]{1,0:T(8,128)(2,1)}), bf16[2048,768]{1,0:T(8,128)(2,1)}) %all-gather.9.cloned.1.call-update) | async-done | bytes 3145744 | tf_op jit(solution)/shard_map/all_gather | solution.py:154
  540.6 9.8 convert_reduce_fusion.1
  556.7 109.5 %reduce-scatter.9.cloned.1.call-done = f32[512,768]{1,0:T(8,128)} async-done(((f32[2048,768]{1,0:T(8,128)}), f32[512,768]{1,0:T(8,128)}) %reduce-scatter.9.cloned.1.call-update) | async-done | bytes 1572880 | tf_op jit(solution)/shard_map/reduce_scatter | solution.py:164
  673.7 63.5 %all-gather.11.cloned.1.call-done = bf16[2048,768]{1,0:T(8,128)(2,1)} async-done(((bf16[512,768]{1,0:T(8,128)(2,1)}), bf16[2048,768]{1,0:T(8,128)(2,1)}) %all-gather.11.cloned.1.call-update) | async-done | bytes 3145744 | tf_op jit(solution)/shard_map/all_gather | solution.py:171
  742.9 12.0 %fusion.21 = f32[32,3,64,64]{2,3,1,0:T(8,128)} fusion(f32[32,3,64,64]{2,3,1,0:T(8,128)} %copy-done.21, f32[32,64,64]{1,2,0:T(8,128)S(1)} %copy-done.12, f32[1,32,64,3,64]{2,1,4,3,0:T(8,128)} %reshape.798, f32[32,64,3]{1,2,0:T(4,128)S(1)} %copy-done.42), kind=kOutput, calls=%fused_computation.38 | convolution fusion | flops 302776320 | bytes 5267456 | tf_op jit(solution)/shard_map/transpose(jvp(vmap(bhij,bjhd->bihd)))/dot_general | solution.py:48
  754.9 7.4 fusion.19
  777.2 8.3 fusion.42
  795.2 7.7 fusion.13
  802.9 7.0 fusion.38
  814.7 8.1 add_bitcast_fusion
  828.5 7.4 copy.171
  835.9 6.7 convert_element_type.170
  847.0 7.1 fusion.108
  864.5 43.0 %all-reduce.3 = (f32[768]{0:T(1024)}, f32[768]{0:T(1024)}, f32[768]{0:T(1024)}, f32[768]{0:T(1024)}, f32[768]{0:T(1024)}, /*index=5*/f32[768]{0:T(1024)}) all-reduce(f32[768]{0:T(1024)S(1)} %copy-done.71, f32[768]{0:T(1024)S(1)} %copy-done.72, f32[768]{0:T(1024)S(1)} %copy-done.73, ...), channel_id=1, replica_groups=mesh['dp'=8,'tensor'=4] {'dp','tensor'}, use_global_device_ids=true, to_apply=%region_22.23 | all-reduce | flops 4608 | bytes 36864 | tf_op jit(solution)/shard_map/psum | solution.py:194
  907.5 14.0 %all-reduce.4 = (f32[576]{0:T(1024)}, f32[768]{0:T(1024)}) all-reduce(f32[576]{0:T(1024)S(1)} %reduce_sum.223, f32[768]{0:T(1024)S(1)} %copy-done.76), channel_id=1, replica_groups=mesh['dp'=8,'tensor'=4] {'dp'}, use_global_device_ids=true, to_apply=%region_19.20 | all-reduce | flops 1344 | bytes 10752 | tf_op jit(solution)/shard_map/psum | solution.py:191
  923.8 101.3 %all-reduce.8.cloned.1.call-done = (f32[768,576]{0,1:T(8,128)}, f32[192,768]{1,0:T(8,128)}, f32[768,768]{1,0:T(8,128)}, f32[768,768]{1,0:T(8,128)}) async-done(((f32[768,576]{0,1:T(8,128)}, f32[192,768]{1,0:T(8,128)}, f32[768,768]{1,0:T(8,128)}, f32[768,768]{1,0:T(8,128)}), (f32[768,576]{0,1:T(8,128)}, f32[192,768]{1,0:T(8,128)}, f32[768,768]{1,0:T(8,128)}, ...) | async-done | bytes 7077904 | tf_op jit(solution)/shard_map/psum | solution.py:191
  (289 shorter events, 170.7 us)
Async XLA Ops:
  7.2 337.2 %copy-start = (bf16[768,768]{1,0:T(8,128)(2,1)S(1)}, bf16[768,768]{1,0:T(8,128)(2,1)}, u32[]{:S(2)}) copy-start(bf16[768,768]{1,0:T(8,128)(2,1)} %param.23) | copy-start | bytes 3538948
  7.2 68.6 %all-gather.5.cloned.1.call-start = ((), (), s32[]{:S(2)}) async-start(), calls=%async_computation.4 | async-start | bytes 3932160 | tf_op jit(solution)/shard_map/all_gather | solution.py:132
  7.9 268.9 %reduce-scatter.5.cloned.1.call-start = ((), (), s32[]{:S(2)}) async-start(), calls=%async_computation.5 | async-start | bytes 7864320 | tf_op jit(solution)/shard_map/reduce_scatter | solution.py:135
  12.1 117.7 %copy-start.61 = (s32[32]{0:T(128)}, s32[32]{0:T(128)S(1)}, u32[]{:S(2)}) copy-start(s32[32]{0:T(128)S(1)} %get-tuple-element.20) | copy-start | bytes 388
  12.1 117.7 %copy-start.64 = (s32[32]{0:T(128)}, s32[32]{0:T(128)S(1)}, u32[]{:S(2)}) copy-start(s32[32]{0:T(128)S(1)} %get-tuple-element.21) | copy-start | bytes 388
  12.2 109.0 %copy-start.39 = (f32[32,64]{1,0:T(8,128)}, f32[32,64]{1,0:T(8,128)S(1)}, u32[]{:S(2)}) copy-start(f32[32,64]{1,0:T(8,128)S(1)} %get-tuple-element.57) | copy-start | bytes 24580
  12.3 98.5 %copy-start.44 = (f32[32,64]{1,0:T(8,128)}, f32[32,64]{1,0:T(8,128)S(1)}, u32[]{:S(2)}) copy-start(f32[32,64]{1,0:T(8,128)S(1)} %get-tuple-element.71) | copy-start | bytes 24580
  12.3 98.4 %copy-start.46 = (f32[32,64]{1,0:T(8,128)}, f32[32,64]{1,0:T(8,128)S(1)}, u32[]{:S(2)}) copy-start(f32[32,64]{1,0:T(8,128)S(1)} %get-tuple-element.72) | copy-start | bytes 24580
  12.7 131.7 %copy-start.11 = (f32[32,64,64]{1,2,0:T(8,128)}, f32[32,64,64]{1,2,0:T(8,128)S(1)}, u32[]{:S(2)}) copy-start(f32[32,64,64]{1,2,0:T(8,128)S(1)} %and_convert_fusion) | copy-start | bytes 1572868
  167.2 109.6 %copy-start.27 = (bf16[512,768]{1,0:T(8,128)(2,1)S(1)}, bf16[512,768]{1,0:T(8,128)(2,1)}, u32[]{:S(2)}) copy-start(bf16[512,768]{1,0:T(8,128)(2,1)} %param.15) | copy-start | bytes 2359300
  167.3 177.1 %all-gather.7.cloned.1.call-start = ((), (), s32[]{:S(2)}) async-start(), calls=%async_computation.6 | async-start | bytes 3932160 | tf_op jit(solution)/shard_map/all_gather | solution.py:140
  278.6 74.1 %copy-start.50 = (f32[512]{0:T(512)}, f32[512]{0:T(512)S(1)}, u32[]{:S(2)}) copy-start(f32[512]{0:T(512)S(1)} %broadcast_multiply_fusion.1) | copy-start | bytes 6148
  278.9 73.8 %copy-start.57 = (f32[512]{0:T(512)}, f32[512]{0:T(512)S(1)}, u32[]{:S(2)}) copy-start(f32[512]{0:T(512)S(1)} %multiply_reduce_fusion.5) | copy-start | bytes 6148
  280.2 188.3 %reduce-scatter.7.cloned.1.call-start = ((), (), s32[]{:S(2)}) async-start(), calls=%async_computation.7 | async-start | bytes 7864320 | tf_op jit(solution)/shard_map/reduce_scatter | solution.py:143
  358.9 181.8 %all-gather.9.cloned.1.call-start = ((), (), s32[]{:S(2)}) async-start(), calls=%async_computation.8 | async-start | bytes 3932160 | tf_op jit(solution)/shard_map/all_gather | solution.py:154
  361.3 109.5 %copy-start.26 = (bf16[512,768]{1,0:T(8,128)(2,1)S(1)}, bf16[512,768]{1,0:T(8,128)(2,1)}, u32[]{:S(2)}) copy-start(bf16[512,768]{1,0:T(8,128)(2,1)} %param.29) | copy-start | bytes 2359300
  476.4 189.7 %reduce-scatter.9.cloned.1.call-start = ((), (), s32[]{:S(2)}) async-start(), calls=%async_computation.9 | async-start | bytes 7864320 | tf_op jit(solution)/shard_map/reduce_scatter | solution.py:164
  556.6 109.6 %copy-start.49 = (f32[768]{0:T(1024)S(1)}, f32[768]{0:T(1024)}, u32[]{:S(2)}) copy-start(f32[768]{0:T(1024)} %convert_element_type.155) | copy-start | bytes 9220
  556.6 109.6 %copy-start.51 = (f32[512]{0:T(512)S(1)}, f32[512]{0:T(512)}, u32[]{:S(2)}) copy-start(f32[512]{0:T(512)} %copy-done.50) | copy-start | bytes 6148
  556.6 109.6 %copy-start.54 = (f32[512]{0:T(512)S(1)}, f32[512]{0:T(512)}, u32[]{:S(2)}) copy-start(f32[512]{0:T(512)} %copy-done.53) | copy-start | bytes 6148
  556.6 112.9 %copy-start.58 = (f32[512]{0:T(512)S(1)}, f32[512]{0:T(512)}, u32[]{:S(2)}) copy-start(f32[512]{0:T(512)} %copy-done.57) | copy-start | bytes 6148
  556.6 180.5 %all-gather.11.cloned.1.call-start = ((), (), s32[]{:S(2)}) async-start(), calls=%async_computation.10 | async-start | bytes 3932160 | tf_op jit(solution)/shard_map/all_gather | solution.py:171
  673.0 248.5 %reduce-scatter.11.cloned.1.call-start = ((), (), s32[]{:S(2)}) async-start(), calls=%async_computation.11 | async-start | bytes 3932160 | tf_op jit(solution)/shard_map/reduce_scatter | solution.py:183
  846.7 178.4 %all-reduce.8.cloned.1.call-start = ((), (), s32[]{:S(2)}) async-start(), calls=%async_computation.12 | async-start | bytes 14155776 | tf_op jit(solution)/shard_map/psum | solution.py:191
  (76 other events, 865.4 us)
Sparse Core Ops, SparseCore 0:
  9.6 66.1 all-gather.4
  167.4 109.3 reduce-scatter.4
  280.3 64.0 all-gather.6
  359.0 109.3 reduce-scatter.6
  476.6 64.0 all-gather.8
  556.7 109.3 reduce-scatter.8
  673.1 64.0 all-gather.10
  846.8 59.8 reduce-scatter.10
  911.5 113.5 all-reduce.7
where the time goes:
time: 1050 us; the launch traced here: 1040 us
  waiting for transfers between devices  681 us (65%)
  matrix products  166 us (16%)
  local copies, waits for them, and re-layouts  73.7 us (7%)
  blocking collectives  57 us (5%)
  other arithmetic  45.5 us (4%)
  between operations  15.3 us (1%)
    reduce_scatter x1, waiting for transfers between devices, on_device(): lax.psum_scatter(rows_back(d_hidden, w_in), 'tensor', scatter_dimension=0...  109 us
    reduce_scatter x1, waiting for transfers between devices, on_device(): lax.psum_scatter(rows_product(attended, w_out), 'tensor', scatter_dimensi...  107 us
    reduce_scatter x1, waiting for transfers between devices, on_device(): lax.psum_scatter(rows_product(active, w_two), 'tensor', scatter_dimension...  107 us
    psum x1, waiting for transfers between devices, on_device(): lax.psum((d_w_qkv, d_b_qkv, d_w_out, d_w_in, d_b_in, d_w_two), 'dp')  101 us
    all_gather x1, waiting for transfers between devices, on_device(): second_full = lax.all_gather(d_second, 'tensor', axis=0, tiled=True)  64.1 us
    all_gather x1, waiting for transfers between devices, on_device(): middle_full = lax.all_gather(first_low, 'tensor', axis=0, tiled=True)  64.1 us
    all_gather x1, waiting for transfers between devices, on_device(): branch_full = lax.all_gather(d_branch, 'tensor', axis=0, tiled=True)  63.5 us
    all_gather x1, waiting for transfers between devices, on_device(): input_full = lax.all_gather(tokens, 'tensor', axis=0, tiled=True)  63.1 us
  transfers between devices with their start and end apart: 9, of which 8 were waited for; matrix products, arithmetic and copies ran while one was open for 3% of the time, Pallas kernels for 0%

commit v1 on v0

--- a/solution.py
+++ b/solution.py
@@ -192,7 +192,8 @@
         (d_w_qkv, d_b_qkv, d_w_out, d_w_in, d_b_in, d_w_two), "dp"
     )
     d_b_out, d_gain_one, d_shift_one, d_b_two, d_gain_two, d_shift_two = lax.psum(
-        (d_b_out, d_gain_one, d_shift_one, d_b_two, d_gain_two, d_shift_two), ("dp", "tensor")
+        lax.psum((d_b_out, d_gain_one, d_shift_one, d_b_two, d_gain_two, d_shift_two), "tensor"),
+        "dp",
     )
     return (
         block_out,

time: 1050 us -> 1040 us (level)
  blocking collectives: 57 us -> 43.7 us
  waiting for transfers between devices: 681 us -> 694 us
    psum x1, blocking collectives: 43 us -> 19.9 us  [on_device(): lax.psum((d_b_out, d_gain_one, d_shift_one, d_b_two, d_gain_two, d_shift_...]
    psum x1, waiting for transfers between devices: 101 us -> 115 us  [on_device(): lax.psum((d_w_qkv, d_b_qkv, d_w_out, d_w_in, d_b_in, d_w_two), 'dp')]
where the time goes in v1:
time: 1040 us
  waiting for transfers between devices  694 us (67%)
  matrix products  166 us (16%)
  local copies, waits for them, and re-layouts  73.7 us (7%)
  other arithmetic  45.5 us (4%)
  blocking collectives  43.7 us (4%)
  between operations  15.3 us (1%)
    psum x1, waiting for transfers between devices, on_device(): lax.psum((d_w_qkv, d_b_qkv, d_w_out, d_w_in, d_b_in, d_w_two), 'dp')  115 us
    reduce_scatter x1, waiting for transfers between devices, on_device(): lax.psum_scatter(rows_back(d_hidden, w_in), 'tensor', scatter_dimension=0...  109 us
    reduce_scatter x1, waiting for transfers between devices, on_device(): lax.psum_scatter(rows_product(attended, w_out), 'tensor', scatter_dimensi...  107 us
    reduce_scatter x1, waiting for transfers between devices, on_device(): lax.psum_scatter(rows_product(active, w_two), 'tensor', scatter_dimension...  107 us
    all_gather x1, waiting for transfers between devices, on_device(): second_full = lax.all_gather(d_second, 'tensor', axis=0, tiled=True)  64.1 us
    all_gather x1, waiting for transfers between devices, on_device(): middle_full = lax.all_gather(first_low, 'tensor', axis=0, tiled=True)  64.1 us
    all_gather x1, waiting for transfers between devices, on_device(): branch_full = lax.all_gather(d_branch, 'tensor', axis=0, tiled=True)  63.5 us
    all_gather x1, waiting for transfers between devices, on_device(): input_full = lax.all_gather(tokens, 'tensor', axis=0, tiled=True)  63.1 us
  transfers between devices with their start and end apart: 9, of which 8 were waited for; matrix products, arithmetic and copies ran while one was open for 3% of the time, Pallas kernels for 0%

profile of v1, /device:TPU:0, one launch (start us, length us, event | category | flops | bytes accessed | tf_op | source)
XLA Modules:
  0.0 1038.6 jit_solution(8130398211555783654)
XLA Ops:
  12.7 63.1 %all-gather.5.cloned.1.call-done = bf16[2048,768]{1,0:T(8,128)(2,1)} async-done(((bf16[512,768]{1,0:T(8,128)(2,1)}), bf16[2048,768]{1,0:T(8,128)(2,1)}) %all-gather.5.cloned.1.call-update) | async-done | bytes 3145744 | tf_op jit(solution)/shard_map/all_gather | solution.py:132
  82.2 8.7 reshape_reshape.3
  90.9 8.2 fusion.101
  150.5 9.1 divide_convert_fusion
  169.7 107.1 %reduce-scatter.5.cloned.1.call-done = f32[512,768]{1,0:T(8,128)} async-done(((f32[2048,768]{1,0:T(8,128)}), f32[512,768]{1,0:T(8,128)}) %reduce-scatter.5.cloned.1.call-update) | async-done | bytes 1572880 | tf_op jit(solution)/shard_map/reduce_scatter | solution.py:135
  280.2 64.1 %all-gather.7.cloned.1.call-done = bf16[2048,768]{1,0:T(8,128)(2,1)} async-done(((bf16[512,768]{1,0:T(8,128)(2,1)}), bf16[2048,768]{1,0:T(8,128)(2,1)}) %all-gather.7.cloned.1.call-update) | async-done | bytes 3145744 | tf_op jit(solution)/shard_map/all_gather | solution.py:140
  344.3 8.4 multiply_convert_fusion
  361.3 107.1 %reduce-scatter.7.cloned.1.call-done = f32[512,768]{1,0:T(8,128)} async-done(((f32[2048,768]{1,0:T(8,128)}), f32[512,768]{1,0:T(8,128)}) %reduce-scatter.7.cloned.1.call-update) | async-done | bytes 1572880 | tf_op jit(solution)/shard_map/reduce_scatter | solution.py:143
  476.5 64.1 %all-gather.9.cloned.1.call-done = bf16[2048,768]{1,0:T(8,128)(2,1)} async-done(((bf16[512,768]{1,0:T(8,128)(2,1)}), bf16[2048,768]{1,0:T(8,128)(2,1)}) %all-gather.9.cloned.1.call-update) | async-done | bytes 3145744 | tf_op jit(solution)/shard_map/all_gather | solution.py:154
  540.6 9.8 convert_reduce_fusion.1
  556.6 109.5 %reduce-scatter.9.cloned.1.call-done = f32[512,768]{1,0:T(8,128)} async-done(((f32[2048,768]{1,0:T(8,128)}), f32[512,768]{1,0:T(8,128)}) %reduce-scatter.9.cloned.1.call-update) | async-done | bytes 1572880 | tf_op jit(solution)/shard_map/reduce_scatter | solution.py:164
  673.7 63.5 %all-gather.11.cloned.1.call-done = bf16[2048,768]{1,0:T(8,128)(2,1)} async-done(((bf16[512,768]{1,0:T(8,128)(2,1)}), bf16[2048,768]{1,0:T(8,128)(2,1)}) %all-gather.11.cloned.1.call-update) | async-done | bytes 3145744 | tf_op jit(solution)/shard_map/all_gather | solution.py:171
  742.9 12.0 %fusion.21 = f32[32,3,64,64]{2,3,1,0:T(8,128)} fusion(f32[32,3,64,64]{2,3,1,0:T(8,128)} %copy-done.21, f32[32,64,64]{1,2,0:T(8,128)S(1)} %copy-done.12, f32[1,32,64,3,64]{2,1,4,3,0:T(8,128)} %reshape.798, f32[32,64,3]{1,2,0:T(4,128)S(1)} %copy-done.42), kind=kOutput, calls=%fused_computation.38 | convolution fusion | flops 302776320 | bytes 5267456 | tf_op jit(solution)/shard_map/transpose(jvp(vmap(bhij,bjhd->bihd)))/dot_general | solution.py:48
  754.8 7.4 fusion.19
  777.2 8.3 fusion.42
  795.1 7.7 fusion.13
  802.9 7.0 fusion.38
  814.7 8.1 add_bitcast_fusion
  828.5 7.3 copy.171
  835.8 6.7 convert_element_type.170
  846.9 7.1 fusion.108
  864.4 19.9 %all-reduce.5 = (f32[768]{0:T(1024)S(1)}, f32[768]{0:T(1024)S(1)}, f32[768]{0:T(1024)S(1)}, f32[768]{0:T(1024)S(1)}, f32[768]{0:T(1024)S(1)}, /*index=5*/f32[768]{0:T(1024)S(1)}) all-reduce(f32[768]{0:T(1024)S(1)} %copy-done.71, f32[768]{0:T(1024)S(1)} %copy-done.72, ...), channel_id=1, replica_groups=mesh['dp'=8,'tensor'=4] {'tensor'}, use_global_device_ids=true, to_apply=%region_22.23 | all-reduce | flops 4608 | bytes 36864 | tf_op jit(solution)/shard_map/psum | solution.py:195
  884.4 23.8 %all-reduce.3 = (f32[576]{0:T(1024)}, f32[768]{0:T(1024)}, f32[768]{0:T(1024)}, f32[768]{0:T(1024)}, f32[768]{0:T(1024)}, /*index=5*/f32[768]{0:T(1024)}, f32[768]{0:T(1024)}, f32[768]{0:T(1024)}) all-reduce(f32[576]{0:T(1024)S(1)} %reduce_sum.223, f32[768]{0:T(1024)S(1)} %get-tuple-element.36, ...), channel_id=1, replica_groups=mesh['dp'=8,'tensor'=4] {'dp'}, use_global_device_ids=true, to_apply=%region_19.20 | all-reduce | flops 5952 | bytes 47616 | tf_op jit(solution)/shard_map/psum | solution.py:191
  910.5 114.6 %all-reduce.8.cloned.1.call-done = (f32[768,576]{0,1:T(8,128)}, f32[192,768]{1,0:T(8,128)}, f32[768,768]{1,0:T(8,128)}, f32[768,768]{1,0:T(8,128)}) async-done(((f32[768,576]{0,1:T(8,128)}, f32[192,768]{1,0:T(8,128)}, f32[768,768]{1,0:T(8,128)}, f32[768,768]{1,0:T(8,128)}), (f32[768,576]{0,1:T(8,128)}, f32[192,768]{1,0:T(8,128)}, f32[768,768]{1,0:T(8,128)}, ...) | async-done | bytes 7077904 | tf_op jit(solution)/shard_map/psum | solution.py:191
  (289 shorter events, 170.6 us)
Async XLA Ops:
  7.2 337.1 %copy-start = (bf16[768,768]{1,0:T(8,128)(2,1)S(1)}, bf16[768,768]{1,0:T(8,128)(2,1)}, u32[]{:S(2)}) copy-start(bf16[768,768]{1,0:T(8,128)(2,1)} %param.23) | copy-start | bytes 3538948
  7.2 68.6 %all-gather.5.cloned.1.call-start = ((), (), s32[]{:S(2)}) async-start(), calls=%async_computation.4 | async-start | bytes 3932160 | tf_op jit(solution)/shard_map/all_gather | solution.py:132
  7.9 268.9 %reduce-scatter.5.cloned.1.call-start = ((), (), s32[]{:S(2)}) async-start(), calls=%async_computation.5 | async-start | bytes 7864320 | tf_op jit(solution)/shard_map/reduce_scatter | solution.py:135
  12.1 117.7 %copy-start.61 = (s32[32]{0:T(128)}, s32[32]{0:T(128)S(1)}, u32[]{:S(2)}) copy-start(s32[32]{0:T(128)S(1)} %get-tuple-element.20) | copy-start | bytes 388
  12.1 117.7 %copy-start.64 = (s32[32]{0:T(128)}, s32[32]{0:T(128)S(1)}, u32[]{:S(2)}) copy-start(s32[32]{0:T(128)S(1)} %get-tuple-element.21) | copy-start | bytes 388
  12.2 109.0 %copy-start.39 = (f32[32,64]{1,0:T(8,128)}, f32[32,64]{1,0:T(8,128)S(1)}, u32[]{:S(2)}) copy-start(f32[32,64]{1,0:T(8,128)S(1)} %get-tuple-element.63) | copy-start | bytes 24580
  12.3 98.5 %copy-start.44 = (f32[32,64]{1,0:T(8,128)}, f32[32,64]{1,0:T(8,128)S(1)}, u32[]{:S(2)}) copy-start(f32[32,64]{1,0:T(8,128)S(1)} %get-tuple-element.77) | copy-start | bytes 24580
  12.3 98.4 %copy-start.46 = (f32[32,64]{1,0:T(8,128)}, f32[32,64]{1,0:T(8,128)S(1)}, u32[]{:S(2)}) copy-start(f32[32,64]{1,0:T(8,128)S(1)} %get-tuple-element.78) | copy-start | bytes 24580
  12.7 131.7 %copy-start.11 = (f32[32,64,64]{1,2,0:T(8,128)}, f32[32,64,64]{1,2,0:T(8,128)S(1)}, u32[]{:S(2)}) copy-start(f32[32,64,64]{1,2,0:T(8,128)S(1)} %and_convert_fusion) | copy-start | bytes 1572868
  167.2 109.6 %copy-start.27 = (bf16[512,768]{1,0:T(8,128)(2,1)S(1)}, bf16[512,768]{1,0:T(8,128)(2,1)}, u32[]{:S(2)}) copy-start(bf16[512,768]{1,0:T(8,128)(2,1)} %param.15) | copy-start | bytes 2359300
  167.2 177.1 %all-gather.7.cloned.1.call-start = ((), (), s32[]{:S(2)}) async-start(), calls=%async_computation.6 | async-start | bytes 3932160 | tf_op jit(solution)/shard_map/all_gather | solution.py:140
  278.5 74.1 %copy-start.50 = (f32[512]{0:T(512)}, f32[512]{0:T(512)S(1)}, u32[]{:S(2)}) copy-start(f32[512]{0:T(512)S(1)} %broadcast_multiply_fusion.1) | copy-start | bytes 6148
  278.8 73.8 %copy-start.57 = (f32[512]{0:T(512)}, f32[512]{0:T(512)S(1)}, u32[]{:S(2)}) copy-start(f32[512]{0:T(512)S(1)} %multiply_reduce_fusion.5) | copy-start | bytes 6148
  280.1 188.3 %reduce-scatter.7.cloned.1.call-start = ((), (), s32[]{:S(2)}) async-start(), calls=%async_computation.7 | async-start | bytes 7864320 | tf_op jit(solution)/shard_map/reduce_scatter | solution.py:143
  358.8 181.8 %all-gather.9.cloned.1.call-start = ((), (), s32[]{:S(2)}) async-start(), calls=%async_computation.8 | async-start | bytes 3932160 | tf_op jit(solution)/shard_map/all_gather | solution.py:154
  361.3 109.5 %copy-start.26 = (bf16[512,768]{1,0:T(8,128)(2,1)S(1)}, bf16[512,768]{1,0:T(8,128)(2,1)}, u32[]{:S(2)}) copy-start(bf16[512,768]{1,0:T(8,128)(2,1)} %param.29) | copy-start | bytes 2359300
  476.4 189.7 %reduce-scatter.9.cloned.1.call-start = ((), (), s32[]{:S(2)}) async-start(), calls=%async_computation.9 | async-start | bytes 7864320 | tf_op jit(solution)/shard_map/reduce_scatter | solution.py:164
  556.5 109.6 %copy-start.49 = (f32[768]{0:T(1024)S(1)}, f32[768]{0:T(1024)}, u32[]{:S(2)}) copy-start(f32[768]{0:T(1024)} %convert_element_type.155) | copy-start | bytes 9220
  556.5 109.6 %copy-start.51 = (f32[512]{0:T(512)S(1)}, f32[512]{0:T(512)}, u32[]{:S(2)}) copy-start(f32[512]{0:T(512)} %copy-done.50) | copy-start | bytes 6148
  556.5 109.6 %copy-start.54 = (f32[512]{0:T(512)S(1)}, f32[512]{0:T(512)}, u32[]{:S(2)}) copy-start(f32[512]{0:T(512)} %copy-done.53) | copy-start | bytes 6148
  556.6 112.9 %copy-start.58 = (f32[512]{0:T(512)S(1)}, f32[512]{0:T(512)}, u32[]{:S(2)}) copy-start(f32[512]{0:T(512)} %copy-done.57) | copy-start | bytes 6148
  556.6 180.5 %all-gather.11.cloned.1.call-start = ((), (), s32[]{:S(2)}) async-start(), calls=%async_computation.10 | async-start | bytes 3932160 | tf_op jit(solution)/shard_map/all_gather | solution.py:171
  672.9 235.2 %reduce-scatter.11.cloned.1.call-start = ((), (), s32[]{:S(2)}) async-start(), calls=%async_computation.11 | async-start | bytes 3932160 | tf_op jit(solution)/shard_map/reduce_scatter | solution.py:183
  846.6 178.4 %all-reduce.8.cloned.1.call-start = ((), (), s32[]{:S(2)}) async-start(), calls=%async_computation.12 | async-start | bytes 14155776 | tf_op jit(solution)/shard_map/psum | solution.py:191
  (76 other events, 815.8 us)
Sparse Core Ops, SparseCore 0:
  9.6 66.1 all-gather.4
  167.4 109.3 reduce-scatter.4
  280.2 64.0 all-gather.6
  359.0 109.3 reduce-scatter.6
  476.5 64.0 all-gather.8
  556.7 109.3 reduce-scatter.8
  673.1 64.0 all-gather.10
  846.7 59.9 reduce-scatter.10
  911.5 113.4 all-reduce.7
